TPU v7x, 32 devices: a whole 2x2x4 slice. The times are simulated.
32 devices in a mesh: band: 4 (over y, core), fft: 8 (over z, x).
Axes of the slice: x: 2, y: 2, z: 4, core: 2. Of those that a mesh axis runs over, the one named last changes fastest.
Arguments:
- start_bands: float32 [2, 8, 96, 9216], P(None, 'band', 'fft'), may hold values from -6 to 6
- potential: float32 [96, 96, 96], P(None, None, 'fft'), may hold values from -2 to 1
- half_height: int32 [96, 96], P('fft'), may hold values from -1 to 24, as said below
- lower_bound: float32 [1], replicated, may hold values from 1 to 2
- upper_bound: float32 [1], replicated, may hold values from 14 to 16
- fermi_level: float32 [1], replicated, may hold values from 0 to 2
Outputs:
- filtered_bands: float32 [2, 8, 96, 9216], P(None, 'band', 'fft')
- energies: float32 [8], P('band')
- band_energy: float32 [1], replicated
Inputs may be any that keep to these rules, and one draw needn't show every extreme that they name: Column (x, y) keeps exactly the wave vectors whose z frequency f has |f| <= half_height[x, y]; -1 marks an empty column; the column of x = y = 0 holds 24; every column whose x or y frequency exceeds 96/4 in magnitude is empty.
All inputs are finite; a program needn't handle non-finite values.
Results may differ from a plain program's by a relative error of at most 0.0003.
Values sent between devices are 32-bit elements; how exact they have to be, the bound alone decides.
No kernel may reach another device: no remote copies, remote signals or barrier semaphores. Data moves between devices by JAX's collectives and lax.ppermute only.
A program may use at most 128 MiB of HBM per device.

v0:
```python
import math
import jax
import jax.numpy as jnp
import numpy as np
from jax import lax
from jax.sharding import PartitionSpec as P

DEGREE = 3
KIN_MAX = 12.0
TEMPER = 0.5
HIGHEST = lax.Precision.HIGHEST


def frequency_of(positions, length):
    return jnp.where(positions < length // 2, positions, positions - length)


def dft_tables(row_positions, col_positions, length):
    rows_int = jnp.asarray(row_positions, dtype=jnp.int32)
    cols_int = jnp.asarray(col_positions, dtype=jnp.int32)
    angle = (
        2.0
        * math.pi
        / length
        * (rows_int[:, None] * cols_int[None, :] % length).astype(jnp.float32)
    )
    return (jnp.cos(angle), jnp.sin(angle))


def transform(real_part, imag_part, pattern, tables, parity):
    cosine, sine = tables
    real_cos = jnp.einsum(pattern, real_part, cosine, precision=HIGHEST)
    real_sin = jnp.einsum(pattern, real_part, sine, precision=HIGHEST)
    imag_cos = jnp.einsum(pattern, imag_part, cosine, precision=HIGHEST)
    imag_sin = jnp.einsum(pattern, imag_part, sine, precision=HIGHEST)
    return (real_cos - parity * imag_sin, parity * real_sin + imag_cos)


def pick_box(array, axis, quarter, length):
    lower = lax.slice_in_dim(array, 0, quarter + 1, axis=axis)
    upper = lax.slice_in_dim(array, length - quarter, length, axis=axis)
    return jnp.concatenate([lower, upper], axis=axis)


def place_box(array, axis, quarter, length):
    lower = lax.slice_in_dim(array, 0, quarter + 1, axis=axis)
    upper = lax.slice_in_dim(array, quarter + 1, 2 * quarter + 1, axis=axis)
    shape = list(array.shape)
    shape[axis] = length - 2 * quarter - 1
    middle = jnp.zeros(tuple(shape), jnp.float32)
    return jnp.concatenate([lower, middle, upper], axis=axis)


def packed_operator(field_real, field_imag, potential):
    length = field_real.shape[3]
    quarter = length // 4
    whole = np.arange(length)
    kept = np.concatenate([np.arange(quarter + 1), np.arange(length - quarter, length)])
    box_to_whole = dft_tables(kept, whole, length)
    whole_to_box = dft_tables(whole, kept, length)
    whole_to_whole = dft_tables(whole, whole, length)
    kept_real = pick_box(pick_box(field_real, 2, quarter, length), 3, quarter, length)
    kept_imag = pick_box(pick_box(field_imag, 2, quarter, length), 3, quarter, length)
    z_real, z_imag = transform(kept_real, kept_imag, "bxyk,kn->bxyn", box_to_whole, 1.0)
    x_real = pick_box(
        lax.all_to_all(z_real, "fft", split_axis=3, concat_axis=1, tiled=True), 1, quarter, length
    )
    x_imag = pick_box(
        lax.all_to_all(z_imag, "fft", split_axis=3, concat_axis=1, tiled=True), 1, quarter, length
    )
    lined_real, lined_imag = transform(x_real, x_imag, "bkyz,kn->bnyz", box_to_whole, 1.0)
    space_real, space_imag = transform(lined_real, lined_imag, "bxkz,kn->bxnz", box_to_whole, 1.0)
    space_real = space_real * potential
    space_imag = space_imag * potential
    ready_real, ready_imag = transform(space_real, space_imag, "bxkz,kn->bxnz", whole_to_box, -1.0)
    back_real, back_imag = transform(ready_real, ready_imag, "bkyz,kn->bnyz", whole_to_whole, -1.0)
    line_real = lax.all_to_all(back_real, "fft", split_axis=1, concat_axis=3, tiled=True)
    line_imag = lax.all_to_all(back_imag, "fft", split_axis=1, concat_axis=3, tiled=True)
    final_real, final_imag = transform(line_real, line_imag, "bxyk,kn->bxyn", whole_to_box, -1.0)
    final_real = place_box(place_box(final_real, 3, quarter, length), 2, quarter, length)
    final_imag = place_box(place_box(final_imag, 3, quarter, length), 2, quarter, length)
    return (final_real, final_imag)


def hamiltonian(field_real, field_imag, potential, inside, kinetic):
    length = field_real.shape[3]
    final_real, final_imag = packed_operator(field_real, field_imag, potential)
    scale = 1.0 / float(length**3)
    return (
        inside * (kinetic * field_real + scale * final_real),
        inside * (kinetic * field_imag + scale * final_imag),
    )


def rotation(gram_real, gram_imag, total_bands):
    embedded = jnp.block([[gram_real, -gram_imag], [gram_imag, gram_real]])
    factor = jnp.linalg.cholesky(embedded)
    selector = jnp.eye(2 * total_bands, total_bands, dtype=jnp.float32)
    inverse_cols = lax.linalg.triangular_solve(
        factor, selector, left_side=True, lower=True, transpose_a=True
    )
    return (inverse_cols[:total_bands], inverse_cols[total_bands:])


def correlation(real_rows, imag_rows, cells_total):
    gram_real = (
        jnp.dot(real_rows, real_rows.T, precision=HIGHEST)
        + jnp.dot(imag_rows, imag_rows.T, precision=HIGHEST)
    ) / cells_total
    gram_imag = (
        jnp.dot(real_rows, imag_rows.T, precision=HIGHEST)
        - jnp.dot(imag_rows, real_rows.T, precision=HIGHEST)
    ) / cells_total
    return (gram_real, gram_imag)


def local(start_bands, potential, half_height, lower_bound, upper_bound, fermi_level):
    band_block = start_bands.shape[1]
    x_cells = start_bands.shape[2]
    length = potential.shape[0]
    cells_total = float(length**3)
    offset = lax.axis_index("fft") * x_cells
    freq_all = frequency_of(jnp.arange(length, dtype=jnp.int32), length)
    freq_x = frequency_of(offset + jnp.arange(x_cells, dtype=jnp.int32), length)
    inside = (jnp.abs(freq_all)[None, None, :] <= half_height[:, :, None]).astype(jnp.float32)
    squared = (
        freq_x[:, None, None] ** 2 + freq_all[None, :, None] ** 2 + freq_all[None, None, :] ** 2
    )
    kinetic = KIN_MAX / (length // 4) ** 2 * squared.astype(jnp.float32)

    def apply_h(field):
        return jnp.stack(hamiltonian(field[0], field[1], potential, inside, kinetic))

    shaped = start_bands.reshape(2, band_block, x_cells, length, length)
    center = 0.5 * (upper_bound[0] + lower_bound[0])
    half_width = 0.5 * (upper_bound[0] - lower_bound[0])
    previous = inside * shaped
    current = (apply_h(previous) - center * previous) / half_width
    for degree_step in range(1, DEGREE):
        following = 2.0 * (apply_h(current) - center * current) / half_width - previous
        previous, current = (current, following)
    flattened = current.reshape(2, band_block, x_cells, length * length)
    everything = lax.all_gather(flattened, "band", axis=1, tiled=True)
    total_bands = everything.shape[1]
    real_rows = everything[0].reshape(total_bands, -1)
    imag_rows = everything[1].reshape(total_bands, -1)
    part_real, part_imag = correlation(real_rows, imag_rows, cells_total)
    gram_real, gram_imag = lax.psum((part_real, part_imag), "fft")
    upper_rows, lower_rows = rotation(gram_real, gram_imag, total_bands)
    first_band = lax.axis_index("band") * band_block
    upper_own = lax.dynamic_slice_in_dim(upper_rows, first_band, band_block, 1)
    lower_own = lax.dynamic_slice_in_dim(lower_rows, first_band, band_block, 1)
    rot_real = jnp.dot(upper_own.T, real_rows, precision=HIGHEST) - jnp.dot(
        lower_own.T, imag_rows, precision=HIGHEST
    )
    rot_imag = jnp.dot(upper_own.T, imag_rows, precision=HIGHEST) + jnp.dot(
        lower_own.T, real_rows, precision=HIGHEST
    )
    rotated_flat = jnp.stack([rot_real, rot_imag]).reshape(2, band_block, x_cells, length * length)
    rotated = rotated_flat.reshape(2, band_block, x_cells, length, length)
    applied = apply_h(rotated)
    partial_energy = jnp.sum(rotated * applied, axis=(0, 2, 3, 4)) / cells_total
    energies = lax.psum(partial_energy, "fft")
    weights = jax.nn.sigmoid((fermi_level[0] - energies) / TEMPER)
    weighted = jnp.sum(weights * energies)
    summed = lax.psum(weighted, "band")
    band_energy = (summed / float(band_block * lax.axis_size("band"))).reshape(1)
    return (rotated_flat, energies, band_energy)


def solution(mesh):
    placed = (P(None, "band", "fft", None), P(None, None, "fft"), P("fft", None), P(), P(), P())
    return jax.shard_map(
        local,
        mesh=mesh,
        in_specs=placed,
        out_specs=(P(None, "band", "fft", None), P("band"), P()),
        check_vma=False,
    )
```

profile of v0, /device:TPU:0, one launch (start us, length us, event | category | flops | bytes accessed | tf_op | source)
XLA Modules:
  0.0 820.1 jit_solution(6142604778680343717)
XLA Ops:
  19.5 4.2 reshape.502
  23.6 7.3 all-to-all-start
  37.3 4.2 reshape.504
  44.0 4.3 all-to-all-start.1
  50.1 3.5 reduce.6
  53.6 3.9 reshape.503
  60.9 3.5 reduce.7
  64.4 3.9 reshape.505
  103.5 4.2 reshape.506
  107.6 6.2 all-to-all-start.2
  121.8 4.2 reshape.508
  126.0 6.0 all-to-all-start.3
  138.0 3.9 reshape.507
  149.4 3.5 reduce.8
  152.9 3.9 reshape.509
  179.8 4.2 reshape.510
  184.0 6.0 all-to-all-start.4
  196.5 4.2 reshape.512
  201.1 5.8 all-to-all-start.5
  206.9 3.6 reduce.10
  210.5 3.9 reshape.511
  217.5 3.5 reduce.11
  221.1 3.9 reshape.513
  260.6 4.2 reshape.514
  264.8 6.2 all-to-all-start.6
  277.1 4.2 reshape.516
  281.3 6.0 all-to-all-start.7
  287.3 3.5 reduce.13
  290.9 3.9 reshape.515
  302.4 3.5 reduce.12
  305.9 3.9 reshape.517
  332.4 4.2 reshape.518
  336.6 6.0 all-to-all-start.8
  352.3 4.5 all-to-all-start.9
  393.9 4.2 reshape.522
  398.0 4.5 all-to-all-start.10
  412.2 4.9 all-to-all-start.11
  465.1 5.7 divide_subtract_fusion
  473.4 52.4 %all-gather.2.cloned.1.call-done = f32[2,8,12,9216]{3,0,2,1:T(2,128)} async-done(((f32[2,2,12,9216]{3,0,2,1:T(2,128)}), f32[2,8,12,9216]{3,0,2,1:T(2,128)}) %all-gather.2.cloned.1.call-update) | async-done | bytes 7077904 | tf_op jit(solution)/shard_map/all_gather | solution.py:143
  525.8 10.0 %fusion.1106 = (f32[1,8,12,9216]{3,0,2,1:T(1,128)S(1)}, f32[1,8,12,9216]{3,0,2,1:T(1,128)S(1)}) fusion(f32[2,8,12,9216]{3,0,2,1:T(2,128)} %all-gather.2.cloned.1.call-done), kind=kLoop, calls=%fused_computation.1039 | loop fusion | bytes 14155776 | tf_op jit(solution)/shard_map/slice | solution.py:145
  535.7 8.2 %fusion.78 = f32[8,8]{0,1:T(8,128)S(1)} fusion(f32[1,8,12,9216]{3,0,2,1:T(1,128)S(1)} %get-tuple-element.14), kind=kOutput, calls=%fused_computation.172 | convolution fusion | flops 84934656 | bytes 3539200 | tf_op jit(solution)/shard_map/dot_general | solution.py:107
  543.9 10.0 %fusion.84 = f32[8,8]{0,1:T(8,128)S(1)} fusion(f32[1,8,12,9216]{3,0,2,1:T(1,128)S(1)} %get-tuple-element.15, f32[1,8,12,9216]{3,0,2,1:T(1,128)S(1)} %get-tuple-element.14), kind=kOutput, calls=%fused_computation.174 | convolution fusion | flops 84934656 | bytes 7078144 | tf_op jit(solution)/shard_map/dot_general | solution.py:111
  553.9 3.9 copy.529
  557.8 3.9 copy.528
  561.7 10.0 %fusion.105 = f32[8,8]{0,1:T(8,128)S(1)} fusion(f32[8,8]{0,1:T(8,128)S(1)} %fusion.84, f32[1,8,12,9216]{3,0,2,1:T(1,128)S(1)} %get-tuple-element.15, f32[1,8,12,9216]{3,0,2,1:T(1,128)S(1)} %get-tuple-element.14), kind=kOutput, calls=%fused_computation.179 | convolution fusion | flops 84934784 | bytes 7078400 | tf_op jit(solution)/shard_map/dot_general | solution.py:112
  571.7 8.4 %fusion.97 = f32[8,8]{0,1:T(8,128)S(1)} fusion(f32[8,8]{0,1:T(8,128)S(1)} %fusion.78, f32[1,8,12,9216]{3,0,2,1:T(1,128)S(1)} %get-tuple-element.15), kind=kOutput, calls=%fused_computation.177 | convolution fusion | flops 84934784 | bytes 3539456 | tf_op jit(solution)/shard_map/dot_general | solution.py:108
  580.1 22.0 %all-reduce = (f32[8,8]{0,1:T(8,128)S(1)}, f32[8,8]{0,1:T(8,128)S(1)}) all-reduce(f32[8,8]{0,1:T(8,128)S(1)} %fusion.97, f32[8,8]{0,1:T(8,128)S(1)} %fusion.105), channel_id=1, replica_groups=mesh['band'=4,'fft'=8] {'fft'}, use_global_device_ids=true, to_apply=%region_0.1 | all-reduce | flops 128 | bytes 1024 | tf_op jit(solution)/shard_map/psum | solution.py:148
  606.7 5.3 fusion.752
  620.8 5.3 fusion.754
  626.1 3.6 convolution_subtract_fusion
  640.8 4.2 reshape.526
  645.0 4.1 all-to-all-start.12
  655.6 4.2 reshape.528
  659.8 6.1 all-to-all-start.13
  665.9 3.5 reduce.18
  669.4 3.9 reshape.527
  676.5 3.5 reduce.19
  680.0 3.9 reshape.529
  719.2 4.2 reshape.530
  723.4 6.2 all-to-all-start.14
  735.8 4.2 reshape.532
  740.0 6.0 all-to-all-start.15
  779.7 21.8 %psum.30 = f32[2]{0:T(128)S(1)} all-reduce(f32[2]{0:T(128)S(1)} %broadcast_multiply_fusion), channel_id=1, replica_groups=mesh['band'=4,'fft'=8] {'fft'}, use_global_device_ids=true, to_apply=%region_5.6 | all-reduce | flops 2 | bytes 16 | tf_op jit(solution)/shard_map/psum | solution.py:163
  804.7 6.5 psum.31
  (517 shorter events, 403.3 us)
Async XLA Ops:
  7.2 2.8 copy-start.99
  7.2 2.8 copy-start.98
  11.9 2.6 copy-start.30
  12.0 2.5 copy-start.73
  23.6 20.4 %all-to-all-start = ((f32[8,1,14112]{2,1,0:T(1,128)}), f32[8,1,14112]{2,1,0:T(1,128)}, u32[]{:S(2)}, u32[]{:S(2)}) async-start(f32[8,1,14112]{2,1,0:T(1,128)} %reshape.502), calls=%async_computation | async-start | bytes 909312 | tf_op jit(solution)/shard_map/all_to_all | solution.py:66
  30.9 2.3 copy-start.31
  30.9 2.3 copy-start.44
  30.9 2.3 copy-start.74
  44.0 16.9 %all-to-all-start.1 = ((f32[8,1,14112]{2,1,0:T(1,128)}), f32[8,1,14112]{2,1,0:T(1,128)}, u32[]{:S(2)}, u32[]{:S(2)}) async-start(f32[8,1,14112]{2,1,0:T(1,128)} %reshape.504), calls=%async_computation.1 | async-start | bytes 909312 | tf_op jit(solution)/shard_map/all_to_all | solution.py:69
  75.7 3.2 copy-start.60
  75.7 3.2 copy-start.63
  87.3 2.7 copy-start.89
  107.6 18.4 %all-to-all-start.2 = ((f32[8,1,14112]{2,1,0:T(1,128)}), f32[8,1,14112]{2,1,0:T(1,128)}, u32[]{:S(2)}, u32[]{:S(2)}) async-start(f32[8,1,14112]{2,1,0:T(1,128)} %reshape.506), calls=%async_computation.2 | async-start | bytes 909312 | tf_op jit(solution)/shard_map/all_to_all | solution.py:77
  115.2 2.5 copy-start.37
  126.0 23.4 %all-to-all-start.3 = ((f32[8,1,14112]{2,1,0:T(1,128)}), f32[8,1,14112]{2,1,0:T(1,128)}, u32[]{:S(2)}, u32[]{:S(2)}) async-start(f32[8,1,14112]{2,1,0:T(1,128)} %reshape.508), calls=%async_computation.3 | async-start | bytes 909312 | tf_op jit(solution)/shard_map/all_to_all | solution.py:78
  161.6 2.1 copy-start.34
  161.6 2.1 copy-start.86
  172.4 2.3 copy-start.28
  172.5 2.3 copy-start.68
  172.5 2.2 copy-start.24
  172.6 2.1 copy-start.75
  184.0 17.1 %all-to-all-start.4 = ((f32[8,1,14112]{2,1,0:T(1,128)}), f32[8,1,14112]{2,1,0:T(1,128)}, u32[]{:S(2)}, u32[]{:S(2)}) async-start(f32[8,1,14112]{2,1,0:T(1,128)} %reshape.510), calls=%async_computation.4 | async-start | bytes 909312 | tf_op jit(solution)/shard_map/all_to_all | solution.py:66
  190.0 2.4 copy-start.29
  190.0 2.4 copy-start.46
  190.0 2.4 copy-start.69
  201.1 16.5 %all-to-all-start.5 = ((f32[8,1,14112]{2,1,0:T(1,128)}), f32[8,1,14112]{2,1,0:T(1,128)}, u32[]{:S(2)}, u32[]{:S(2)}) async-start(f32[8,1,14112]{2,1,0:T(1,128)} %reshape.512), calls=%async_computation.5 | async-start | bytes 909312 | tf_op jit(solution)/shard_map/all_to_all | solution.py:69
  232.4 3.2 copy-start.61
  232.4 3.2 copy-start.64
  244.1 2.7 copy-start.90
  264.8 16.6 %all-to-all-start.6 = ((f32[8,1,14112]{2,1,0:T(1,128)}), f32[8,1,14112]{2,1,0:T(1,128)}, u32[]{:S(2)}, u32[]{:S(2)}) async-start(f32[8,1,14112]{2,1,0:T(1,128)} %reshape.514), calls=%async_computation.6 | async-start | bytes 909312 | tf_op jit(solution)/shard_map/all_to_all | solution.py:77
  271.0 2.1 copy-start.40
  281.3 21.1 %all-to-all-start.7 = ((f32[8,1,14112]{2,1,0:T(1,128)}), f32[8,1,14112]{2,1,0:T(1,128)}, u32[]{:S(2)}, u32[]{:S(2)}) async-start(f32[8,1,14112]{2,1,0:T(1,128)} %reshape.516), calls=%async_computation.7 | async-start | bytes 909312 | tf_op jit(solution)/shard_map/all_to_all | solution.py:78
  314.7 2.1 copy-start.35
  314.7 2.1 copy-start.87
  322.7 2.3 copy-start.19
  322.7 2.3 copy-start.21
  336.6 15.7 %all-to-all-start.8 = ((f32[8,1,14112]{2,1,0:T(1,128)}), f32[8,1,14112]{2,1,0:T(1,128)}, u32[]{:S(2)}, u32[]{:S(2)}) async-start(f32[8,1,14112]{2,1,0:T(1,128)} %reshape.518), calls=%async_computation.8 | async-start | bytes 909312 | tf_op jit(solution)/shard_map/all_to_all | solution.py:66
  352.3 13.8 %all-to-all-start.9 = ((f32[8,1,14112]{2,1,0:T(1,128)}), f32[8,1,14112]{2,1,0:T(1,128)}, u32[]{:S(2)}, u32[]{:S(2)}) async-start(f32[8,1,14112]{2,1,0:T(1,128)} %reshape.520), calls=%async_computation.9 | async-start | bytes 909312 | tf_op jit(solution)/shard_map/all_to_all | solution.py:69
  375.1 3.1 copy-start.97
  393.9 8.7 %copy-start.100 = (s32[96]{0:T(128)S(1)}, s32[96]{0:T(128)}, u32[]{:S(2)}) copy-start(s32[96]{0:T(128)} %copy-done.99) | copy-start | bytes 1156
  398.0 14.2 %all-to-all-start.10 = ((f32[8,1,14112]{2,1,0:T(1,128)}), f32[8,1,14112]{2,1,0:T(1,128)}, u32[]{:S(2)}, u32[]{:S(2)}) async-start(f32[8,1,14112]{2,1,0:T(1,128)} %reshape.522), calls=%async_computation.10 | async-start | bytes 909312 | tf_op jit(solution)/shard_map/all_to_all | solution.py:77
  406.7 10.5 %copy-start.93 = (s32[12,9216]{1,0:T(8,128)S(1)}, s32[12,9216]{1,0:T(8,128)}, u32[]{:S(2)}) copy-start(s32[12,9216]{1,0:T(8,128)} %le.38) | copy-start | bytes 1327108
  409.7 8.4 %copy-start.13 = (f32[1,2,12,96,96]{4,3,2,1,0:T(8,128)S(1)}, f32[1,2,12,96,96]{4,3,2,1,0:T(8,128)}, u32[]{:S(2)}) copy-start(f32[1,2,12,96,96]{4,3,2,1,0:T(8,128)} %copy-done.11) | copy-start | bytes 2654212
  412.2 28.9 %all-to-all-start.11 = ((f32[8,1,14112]{2,1,0:T(1,128)}), f32[8,1,14112]{2,1,0:T(1,128)}, u32[]{:S(2)}, u32[]{:S(2)}) async-start(f32[8,1,14112]{2,1,0:T(1,128)} %reshape.524), calls=%async_computation.11 | async-start | bytes 909312 | tf_op jit(solution)/shard_map/all_to_all | solution.py:78
  417.2 108.6 %all-gather.2.cloned.1.call-start = ((), (), s32[]{:S(2)}) async-start(), calls=%async_computation.16 | async-start | bytes 8847360 | tf_op jit(solution)/shard_map/all_gather | solution.py:143
  446.9 2.5 copy-start.88
  461.3 3.8 copy-start.92
  463.0 2.1 copy-start.23
  606.7 5.3 copy-start.1
  620.8 5.3 copy-start
  632.6 3.1 copy-start.25
  645.0 14.9 %all-to-all-start.12 = ((f32[8,1,14112]{2,1,0:T(1,128)}), f32[8,1,14112]{2,1,0:T(1,128)}, u32[]{:S(2)}, u32[]{:S(2)}) async-start(f32[8,1,14112]{2,1,0:T(1,128)} %reshape.526), calls=%async_computation.12 | async-start | bytes 909312 | tf_op jit(solution)/shard_map/all_to_all | solution.py:66
  649.1 2.4 copy-start.27
  649.1 2.4 copy-start.48
  649.1 2.4 copy-start.67
  659.8 16.7 %all-to-all-start.13 = ((f32[8,1,14112]{2,1,0:T(1,128)}), f32[8,1,14112]{2,1,0:T(1,128)}, u32[]{:S(2)}, u32[]{:S(2)}) async-start(f32[8,1,14112]{2,1,0:T(1,128)} %reshape.528), calls=%async_computation.13 | async-start | bytes 909312 | tf_op jit(solution)/shard_map/all_to_all | solution.py:69
  691.3 3.2 copy-start.62
  691.4 3.2 copy-start.65
  702.9 2.7 copy-start.91
  723.4 16.6 %all-to-all-start.14 = ((f32[8,1,14112]{2,1,0:T(1,128)}), f32[8,1,14112]{2,1,0:T(1,128)S(1)}, u32[]{:S(2)}, u32[]{:S(2)}) async-start(f32[8,1,14112]{2,1,0:T(1,128)} %reshape.530), calls=%async_computation.14 | async-start | bytes 909312 | tf_op jit(solution)/shard_map/all_to_all | solution.py:77
  729.6 2.1 copy-start.42
  740.0 8.5 %copy-start.94 = (f32[8,1,14112]{2,1,0:T(1,128)}, f32[8,1,14112]{2,1,0:T(1,128)S(1)}, u32[]{:S(2)}) copy-start(f32[8,1,14112]{2,1,0:T(1,128)S(1)} %all-to-all-done.14) | copy-start | bytes 1354756
  740.0 22.0 %all-to-all-start.15 = ((f32[8,1,14112]{2,1,0:T(1,128)}), f32[8,1,14112]{2,1,0:T(1,128)}, u32[]{:S(2)}, u32[]{:S(2)}) async-start(f32[8,1,14112]{2,1,0:T(1,128)} %reshape.532), calls=%async_computation.15 | async-start | bytes 909312 | tf_op jit(solution)/shard_map/all_to_all | solution.py:78
  801.5 3.2 copy-start.101
  (55 other events, 75.1 us)
Sparse Core Ops, SparseCore 0:
  473.5 52.2 all-gather.1
where the time goes:
time: 834 us; the launch traced here: 820 us
  local copies, waits for them, and re-layouts  328 us (39%)
  matrix products  194 us (23%)
  starting transfers between devices  90.2 us (11%)
  other arithmetic  73.5 us (9%)
  waiting for transfers between devices  63.7 us (8%)
  blocking collectives  50.4 us (6%)
  between operations  20.3 us (2%)
    unnamed x256, local copies, waits for them, and re-layouts  181 us
    all_gather x1, waiting for transfers between devices, local(): everything = lax.all_gather(flattened, 'band', axis=1, tiled=True)  52.4 us
    dot_general x24, matrix products, transform(): real_sin = jnp.einsum(pattern, real_part, sine, precision=HIGHEST)  44.5 us
    dot_general x24, matrix products, transform(): imag_sin = jnp.einsum(pattern, imag_part, sine, precision=HIGHEST)  35.1 us
    dot_general x24, matrix products, transform(): imag_cos = jnp.einsum(pattern, imag_part, cosine, precision=HIGHEST)  30.3 us
    dot_general x24, matrix products, transform(): real_cos = jnp.einsum(pattern, real_part, cosine, precision=HIGHEST)  29.4 us
    all_to_all x4, starting transfers between devices, packed_operator(): lax.all_to_all(z_real, 'fft', split_axis=3, concat_axis=1, tiled=True)  23.4 us
    all_to_all x4, starting transfers between devices, packed_operator(): lax.all_to_all(back_real, 'fft', split_axis=1, concat_axis=3, tiled=True)  23.1 us
  transfers between devices with their start and end apart: 17, of which 7 were waited for; matrix products, arithmetic and copies ran while one was open for 23% of the time, Pallas kernels for 0%

commit v1 on v0

--- a/solution.py
+++ b/solution.py
@@ -140,7 +140,7 @@
         following = 2.0 * (apply_h(current) - center * current) / half_width - previous
         previous, current = (current, following)
     flattened = current.reshape(2, band_block, x_cells, length * length)
-    everything = lax.all_gather(flattened, "band", axis=1, tiled=True)
+    everything = jnp.concatenate(lax.all_gather(flattened, "band"), axis=1)
     total_bands = everything.shape[1]
     real_rows = everything[0].reshape(total_bands, -1)
     imag_rows = everything[1].reshape(total_bands, -1)

time: 834 us -> 786 us (0.942)
  local copies, waits for them, and re-layouts: 328 us -> 286 us
  matrix products: 194 us -> 178 us
  waiting for transfers between devices: 63.7 us -> 78.5 us
    unnamed x256 -> x240, local copies, waits for them, and re-layouts: 181 us -> 161 us
    slice x1, local copies, waits for them, and re-layouts: 9.97 us -> 1.01 us  [local(): real_rows = everything[0].reshape(total_bands, -1)]
  transfers between devices with their start and end apart: 17 -> 17, of which waited for: 7 -> 10; matrix products, arithmetic and copies ran while one was open for 23% -> 22% of each run, Pallas kernels for 0% -> 0%
where the time goes in v1:
time: 786 us; the launch traced here: 773 us
  local copies, waits for them, and re-layouts  286 us (36%)
  matrix products  178 us (23%)
  starting transfers between devices  83.9 us (11%)
  waiting for transfers between devices  78.5 us (10%)
  other arithmetic  74.5 us (9%)
  blocking collectives  50.6 us (6%)
  between operations  20.7 us (3%)
    unnamed x240, local copies, waits for them, and re-layouts  161 us
    all_gather x1, waiting for transfers between devices, local(): everything = jnp.concatenate(lax.all_gather(flattened, 'band'), axis=1)  52.4 us
    dot_general x24, matrix products, transform(): real_sin = jnp.einsum(pattern, real_part, sine, precision=HIGHEST)  39.6 us
    dot_general x24, matrix products, transform(): imag_sin = jnp.einsum(pattern, imag_part, sine, precision=HIGHEST)  32.6 us
    dot_general x24, matrix products, transform(): real_cos = jnp.einsum(pattern, real_part, cosine, precision=HIGHEST)  28.5 us
    dot_general x24, matrix products, transform(): imag_cos = jnp.einsum(pattern, imag_part, cosine, precision=HIGHEST)  28.2 us
    all_to_all x4, starting transfers between devices, packed_operator(): lax.all_to_all(z_real, 'fft', split_axis=3, concat_axis=1, tiled=True)  23.4 us
    psum x1, blocking collectives, local(): gram_real, gram_imag = lax.psum((part_real, part_imag), 'fft')  22.3 us
  transfers between devices with their start and end apart: 17, of which 10 were waited for; matrix products, arithmetic and copies ran while one was open for 22% of the time, Pallas kernels for 0%

profile of v1, /device:TPU:0, one launch (start us, length us, event | category | flops | bytes accessed | tf_op | source)
XLA Modules:
  0.0 772.6 jit_solution(5706729185562711395)
XLA Ops:
  19.5 4.2 reshape.520
  23.7 7.3 all-to-all-start
  37.4 4.2 reshape.522
  44.1 4.3 all-to-all-start.1
  50.3 3.5 reduce.6
  53.8 3.9 reshape.521
  60.9 3.5 reduce.7
  64.4 3.9 reshape.523
  75.8 3.2 fusion.84
  103.7 4.2 reshape.524
  107.9 6.0 all-to-all-start.2
  121.9 4.2 reshape.526
  126.1 6.0 all-to-all-start.3
  134.5 3.5 reduce.9
  138.0 3.9 reshape.525
  149.5 3.5 reduce.8
  153.0 3.9 reshape.527
  179.9 4.2 reshape.528
  184.1 6.0 all-to-all-start.4
  196.6 4.2 reshape.530
  201.2 5.9 all-to-all-start.5
  207.1 3.5 reduce.10
  210.7 3.9 reshape.529
  217.7 3.6 reduce.11
  221.3 3.9 reshape.531
  232.6 3.2 fusion.82
  260.4 4.2 reshape.532
  264.6 6.3 all-to-all-start.6
  277.1 4.2 reshape.534
  281.3 6.0 all-to-all-start.7
  287.3 3.5 reduce.13
  290.8 3.9 reshape.533
  302.2 3.6 reduce.12
  305.7 3.9 reshape.535
  332.3 4.2 reshape.536
  336.5 6.0 all-to-all-start.8
  349.2 3.0 all-to-all-done.8
  352.2 4.3 all-to-all-start.9
  398.0 4.5 all-to-all-start.10
  412.2 5.0 all-to-all-start.11
  460.6 6.8 divide_subtract_fusion
  467.4 52.4 %all-gather.3.cloned.1.call-done = f32[8,2,12,9216]{3,1,2,0:T(2,128)} async-done(((f32[2,2,12,9216]{3,1,2,0:T(2,128)}), f32[8,2,12,9216]{3,1,2,0:T(2,128)}) %all-gather.3.cloned.1.call-update) | async-done | bytes 7077904 | tf_op jit(solution)/shard_map/all_gather | solution.py:143
  519.8 5.3 copy.533
  530.2 7.6 fusion.1062
  537.9 8.1 %fusion.1063 = f32[8,8]{0,1:T(8,128)S(1)} fusion(f32[8,110592]{1,0:T(8,128)S(1)} %bitcast.558, f32[8,110592]{1,0:T(8,128)S(1)} %bitcast.552), kind=kOutput, calls=%fused_computation.1023 | convolution fusion | flops 84934656 | bytes 7078144 | tf_op jit(solution)/shard_map/dot_general | solution.py:111
  546.0 8.3 %fusion.68 = f32[8,8]{0,1:T(8,128)} fusion(f32[8,8]{0,1:T(8,128)S(1)} %fusion.1063, f32[8,110592]{1,0:T(8,128)S(1)} %bitcast.553, f32[8,110592]{1,0:T(8,128)S(1)} %bitcast.559), kind=kOutput, calls=%fused_computation.164 | convolution fusion | flops 84934784 | bytes 7078400 | tf_op jit(solution)/shard_map/dot_general | solution.py:112
  554.3 8.6 %fusion.69 = f32[8,8]{0,1:T(8,128)} fusion(f32[8,8]{0,1:T(8,128)S(1)} %fusion.1062, f32[8,110592]{1,0:T(8,128)S(1)} %bitcast.554), kind=kOutput, calls=%fused_computation.166 | convolution fusion | flops 84934784 | bytes 3539456 | tf_op jit(solution)/shard_map/dot_general | solution.py:108
  563.0 22.3 %all-reduce = (f32[8,8]{0,1:T(8,128)}, f32[8,8]{0,1:T(8,128)S(1)}) all-reduce(f32[8,8]{0,1:T(8,128)} %fusion.69, f32[8,8]{0,1:T(8,128)S(1)} %copy-done.90), channel_id=1, replica_groups=mesh['band'=4,'fft'=8] {'fft'}, use_global_device_ids=true, to_apply=%region_0.1 | all-reduce | flops 128 | bytes 1024 | tf_op jit(solution)/shard_map/psum | solution.py:148
  595.7 3.2 fusion.712
  598.9 4.3 convolution_add_fusion
  603.2 3.0 squeeze.38
  609.7 5.1 fusion.714
  614.8 4.0 convolution_subtract_fusion
  624.7 4.2 reshape.544
  628.9 4.1 all-to-all-start.12
  638.7 4.3 all-to-all-done.12
  643.0 4.1 all-to-all-start.13
  652.9 4.2 all-to-all-done.13
  681.7 3.9 all-to-all-start.14
  688.3 3.0 reshape.550
  691.2 6.1 all-to-all-done.14
  697.4 4.1 all-to-all-start.15
  732.0 21.8 %psum.30 = f32[2]{0:T(128)S(1)} all-reduce(f32[2]{0:T(128)S(1)} %broadcast_multiply_fusion), channel_id=1, replica_groups=mesh['band'=4,'fft'=8] {'fft'}, use_global_device_ids=true, to_apply=%region_5.6 | all-reduce | flops 2 | bytes 16 | tf_op jit(solution)/shard_map/psum | solution.py:163
  757.0 6.6 psum.31
  (501 shorter events, 372.5 us)
Async XLA Ops:
  7.2 2.8 copy-start.91
  7.2 2.8 copy-start.89
  10.2 441.4 %copy-start.4 = (f32[12,96,96]{2,1,0:T(8,128)}, f32[12,96,96]{2,1,0:T(8,128)S(1)}, u32[]{:S(2)}) copy-start(f32[12,96,96]{2,1,0:T(8,128)S(1)} %compare_convert_fusion.1) | copy-start | bytes 1327108
  12.0 2.6 copy-start.34
  12.0 2.5 copy-start.66
  23.7 20.4 %all-to-all-start = ((f32[8,1,14112]{2,1,0:T(1,128)}), f32[8,1,14112]{2,1,0:T(1,128)}, u32[]{:S(2)}, u32[]{:S(2)}) async-start(f32[8,1,14112]{2,1,0:T(1,128)} %reshape.520), calls=%async_computation | async-start | bytes 909312 | tf_op jit(solution)/shard_map/all_to_all | solution.py:66
  31.0 2.3 copy-start.35
  31.0 2.3 copy-start.46
  31.0 2.3 copy-start.67
  44.1 16.9 %all-to-all-start.1 = ((f32[8,1,14112]{2,1,0:T(1,128)}), f32[8,1,14112]{2,1,0:T(1,128)}, u32[]{:S(2)}, u32[]{:S(2)}) async-start(f32[8,1,14112]{2,1,0:T(1,128)} %reshape.522), calls=%async_computation.1 | async-start | bytes 909312 | tf_op jit(solution)/shard_map/all_to_all | solution.py:69
  49.7 337.7 %copy-start.2 = (f32[96,96,12]{0,1,2:T(8,128)}, f32[96,96,12]{0,1,2:T(8,128)S(1)}, u32[]{:S(2)}) copy-start(f32[96,96,12]{0,1,2:T(8,128)S(1)} %copy.345) | copy-start | bytes 1327108
  75.8 3.2 copy-start.56
  75.8 3.2 copy-start.58
  87.4 2.7 copy-start.81
  96.9 1.9 copy-start.40
  107.9 18.2 %all-to-all-start.2 = ((f32[8,1,14112]{2,1,0:T(1,128)}), f32[8,1,14112]{2,1,0:T(1,128)}, u32[]{:S(2)}, u32[]{:S(2)}) async-start(f32[8,1,14112]{2,1,0:T(1,128)} %reshape.524), calls=%async_computation.2 | async-start | bytes 909312 | tf_op jit(solution)/shard_map/all_to_all | solution.py:77
  115.3 2.5 copy-start.41
  126.1 23.4 %all-to-all-start.3 = ((f32[8,1,14112]{2,1,0:T(1,128)}), f32[8,1,14112]{2,1,0:T(1,128)}, u32[]{:S(2)}, u32[]{:S(2)}) async-start(f32[8,1,14112]{2,1,0:T(1,128)} %reshape.526), calls=%async_computation.3 | async-start | bytes 909312 | tf_op jit(solution)/shard_map/all_to_all | solution.py:78
  161.8 2.1 copy-start.38
  161.8 2.1 copy-start.78
  167.5 1.7 copy-start.7
  172.7 2.3 copy-start.32
  172.7 2.3 copy-start.61
  172.7 2.2 copy-start.30
  172.8 2.1 copy-start.68
  184.1 17.1 %all-to-all-start.4 = ((f32[8,1,14112]{2,1,0:T(1,128)}), f32[8,1,14112]{2,1,0:T(1,128)}, u32[]{:S(2)}, u32[]{:S(2)}) async-start(f32[8,1,14112]{2,1,0:T(1,128)} %reshape.528), calls=%async_computation.4 | async-start | bytes 909312 | tf_op jit(solution)/shard_map/all_to_all | solution.py:66
  190.1 2.4 copy-start.33
  190.1 2.4 copy-start.48
  190.1 2.4 copy-start.62
  201.2 16.5 %all-to-all-start.5 = ((f32[8,1,14112]{2,1,0:T(1,128)}), f32[8,1,14112]{2,1,0:T(1,128)}, u32[]{:S(2)}, u32[]{:S(2)}) async-start(f32[8,1,14112]{2,1,0:T(1,128)} %reshape.530), calls=%async_computation.5 | async-start | bytes 909312 | tf_op jit(solution)/shard_map/all_to_all | solution.py:69
  232.6 3.2 copy-start.57
  232.6 3.2 copy-start.59
  244.3 2.7 copy-start.82
  253.6 1.9 copy-start.43
  264.6 16.7 %all-to-all-start.6 = ((f32[8,1,14112]{2,1,0:T(1,128)}), f32[8,1,14112]{2,1,0:T(1,128)}, u32[]{:S(2)}, u32[]{:S(2)}) async-start(f32[8,1,14112]{2,1,0:T(1,128)} %reshape.532), calls=%async_computation.6 | async-start | bytes 909312 | tf_op jit(solution)/shard_map/all_to_all | solution.py:77
  270.8 2.1 copy-start.44
  281.3 20.9 %all-to-all-start.7 = ((f32[8,1,14112]{2,1,0:T(1,128)}), f32[8,1,14112]{2,1,0:T(1,128)}, u32[]{:S(2)}, u32[]{:S(2)}) async-start(f32[8,1,14112]{2,1,0:T(1,128)} %reshape.534), calls=%async_computation.7 | async-start | bytes 909312 | tf_op jit(solution)/shard_map/all_to_all | solution.py:78
  314.7 2.1 copy-start.39
  314.7 2.1 copy-start.79
  322.0 1.9 copy-start.16
  322.6 2.3 copy-start.25
  322.6 2.3 copy-start.27
  326.4 1.8 copy-start.63
  336.5 15.7 %all-to-all-start.8 = ((f32[8,1,14112]{2,1,0:T(1,128)}), f32[8,1,14112]{2,1,0:T(1,128)}, u32[]{:S(2)}, u32[]{:S(2)}) async-start(f32[8,1,14112]{2,1,0:T(1,128)} %reshape.536), calls=%async_computation.8 | async-start | bytes 909312 | tf_op jit(solution)/shard_map/all_to_all | solution.py:66
  342.5 2.0 copy-start.64
  352.2 13.8 %all-to-all-start.9 = ((f32[8,1,14112]{2,1,0:T(1,128)}), f32[8,1,14112]{2,1,0:T(1,128)}, u32[]{:S(2)}, u32[]{:S(2)}) async-start(f32[8,1,14112]{2,1,0:T(1,128)} %reshape.538), calls=%async_computation.9 | async-start | bytes 909312 | tf_op jit(solution)/shard_map/all_to_all | solution.py:69
  375.0 3.1 copy-start.87
  395.1 7.5 copy-start.92
  398.0 14.2 %all-to-all-start.10 = ((f32[8,1,14112]{2,1,0:T(1,128)}), f32[8,1,14112]{2,1,0:T(1,128)}, u32[]{:S(2)}, u32[]{:S(2)}) async-start(f32[8,1,14112]{2,1,0:T(1,128)} %reshape.540), calls=%async_computation.10 | async-start | bytes 909312 | tf_op jit(solution)/shard_map/all_to_all | solution.py:77
  406.7 10.5 %copy-start.84 = (s32[12,9216]{1,0:T(8,128)S(1)}, s32[12,9216]{1,0:T(8,128)}, u32[]{:S(2)}) copy-start(s32[12,9216]{1,0:T(8,128)} %le.38) | copy-start | bytes 1327108
  409.7 8.5 %copy-start.17 = (f32[1,2,12,96,96]{4,3,2,1,0:T(8,128)S(1)}, f32[1,2,12,96,96]{4,3,2,1,0:T(8,128)}, u32[]{:S(2)}) copy-start(f32[1,2,12,96,96]{4,3,2,1,0:T(8,128)} %copy-done.15) | copy-start | bytes 2654212
  412.2 28.9 %all-to-all-start.11 = ((f32[8,1,14112]{2,1,0:T(1,128)}), f32[8,1,14112]{2,1,0:T(1,128)S(1)}, u32[]{:S(2)}, u32[]{:S(2)}) async-start(f32[8,1,14112]{2,1,0:T(1,128)} %reshape.542), calls=%async_computation.11 | async-start | bytes 909312 | tf_op jit(solution)/shard_map/all_to_all | solution.py:78
  417.2 102.6 %all-gather.3.cloned.1.call-start = ((), (), s32[]{:S(2)}) async-start(), calls=%async_computation.16 | async-start | bytes 8847360 | tf_op jit(solution)/shard_map/all_gather | solution.py:143
  424.8 1.7 copy-start.26
  528.1 17.8 %copy-start = (f32[1,8,12,9216]{3,1,2,0:T(8,128)}, f32[1,8,12,9216]{3,1,2,0:T(8,128)S(1)}, u32[]{:S(2)}) copy-start(f32[1,8,12,9216]{3,1,2,0:T(8,128)S(1)} %copy.525) | copy-start | bytes 10616836
  554.3 8.6 %copy-start.90 = (f32[8,8]{0,1:T(8,128)S(1)}, f32[8,8]{0,1:T(8,128)}, u32[]{:S(2)}) copy-start(f32[8,8]{0,1:T(8,128)} %fusion.68) | copy-start | bytes 772
  595.7 3.2 copy-start.1
  628.9 14.1 %all-to-all-start.12 = ((f32[8,1,14112]{2,1,0:T(1,128)}), f32[8,1,14112]{2,1,0:T(1,128)}, u32[]{:S(2)}, u32[]{:S(2)}) async-start(f32[8,1,14112]{2,1,0:T(1,128)} %reshape.544), calls=%async_computation.12 | async-start | bytes 909312 | tf_op jit(solution)/shard_map/all_to_all | solution.py:66
  643.0 14.1 %all-to-all-start.13 = ((f32[8,1,14112]{2,1,0:T(1,128)}), f32[8,1,14112]{2,1,0:T(1,128)S(1)}, u32[]{:S(2)}, u32[]{:S(2)}) async-start(f32[8,1,14112]{2,1,0:T(1,128)} %reshape.546), calls=%async_computation.13 | async-start | bytes 909312 | tf_op jit(solution)/shard_map/all_to_all | solution.py:69
  681.7 15.6 %all-to-all-start.14 = ((f32[8,1,14112]{2,1,0:T(1,128)}), f32[8,1,14112]{2,1,0:T(1,128)S(1)}, u32[]{:S(2)}, u32[]{:S(2)}) async-start(f32[8,1,14112]{2,1,0:T(1,128)} %reshape.548), calls=%async_computation.14 | async-start | bytes 909312 | tf_op jit(solution)/shard_map/all_to_all | solution.py:77
  688.3 13.9 %copy-start.23 = (f32[2,110592]{1,0:T(2,128)S(1)}, f32[2,110592]{1,0:T(2,128)}, u32[]{:S(2)}) copy-start(f32[2,110592]{1,0:T(2,128)} %convolution_subtract_fusion) | copy-start | bytes 2654212
  697.4 19.5 %all-to-all-start.15 = ((f32[8,1,14112]{2,1,0:T(1,128)}), f32[8,1,14112]{2,1,0:T(1,128)}, u32[]{:S(2)}, u32[]{:S(2)}) async-start(f32[8,1,14112]{2,1,0:T(1,128)} %reshape.550), calls=%async_computation.15 | async-start | bytes 909312 | tf_op jit(solution)/shard_map/all_to_all | solution.py:78
  722.6 2.8 copy-start.77
  753.8 3.2 copy-start.93
  (47 other events, 60.3 us)
Sparse Core Ops, SparseCore 0:
  467.5 52.2 all-gather.2
